TPU v7x, 32 devices: a whole 2x2x4 slice. The times are simulated.
32 devices in a mesh: seq: 16 (over z, x, core), head: 2 (over y).
Axes of the slice: x: 2, y: 2, z: 4, core: 2. Of those that a mesh axis runs over, the one named last changes fastest.
Arguments:
- queries: bfloat16 [2, 1024, 4096], P(None, ('seq', 'head')), may hold values from -6 to 6
- keys: bfloat16 [2, 1024, 4096], P(None, ('seq', 'head')), may hold values from -6 to 6
- values: bfloat16 [2, 1024, 4096], P(None, ('seq', 'head')), may hold values from -6 to 6
- rates: bfloat16 [2, 1024, 8], P(None, ('seq', 'head')), may hold values from 0.049804688 to 1
- fast_init: float32 [8, 3, 512, 256], P('head', None, 'seq'), may hold values from -0.25 to 0.25
Outputs:
- outputs: bfloat16 [2, 1024, 4096], P(None, 'seq', 'head')
All inputs are finite; a program needn't handle non-finite values.
Results may differ from a plain program's by a relative error of at most 0.0085.
Values may be sent and summed in bfloat16 or wider, within the bound.
No kernel may reach another device: no remote copies, remote signals or barrier semaphores. Data moves between devices by JAX's collectives and lax.ppermute only.
A program may use at most 64 MiB of HBM per device.

v0:
```python
import jax
import jax.numpy as jnp
from jax import lax
from jax.sharding import PartitionSpec as P

EPSILON = 1e-06
COEF_A = 3.4445
COEF_B = -4.775
COEF_C = 2.0315
LEARNING_STEP = 0.5
FULL_PRECISION = lax.Precision.HIGHEST


def silu_parts(gate_pre):
    sigmoid_value = jax.nn.sigmoid(gate_pre)
    return (gate_pre * sigmoid_value, sigmoid_value * (1.0 + gate_pre * (1.0 - sigmoid_value)))


def local_gram(weight_matrices):
    return jnp.einsum("hmrf,hmrg->hmfg", weight_matrices, weight_matrices, precision=FULL_PRECISION)


def newton_schulz(gradients, gram_fn):
    gram_matrix = gram_fn(gradients)
    norm_value = jnp.sqrt(jnp.trace(gram_matrix, axis1=2, axis2=3)) + EPSILON
    current_weights = gradients / norm_value[:, :, None, None]
    gram_matrix = gram_matrix / (norm_value * norm_value)[:, :, None, None]
    identity = jnp.eye(gram_matrix.shape[-1], dtype=gram_matrix.dtype)
    for sweeps in range(2):
        if sweeps > 0:
            gram_matrix = gram_fn(current_weights)
        square = jnp.einsum("hmfg,hmgk->hmfk", gram_matrix, gram_matrix, precision=FULL_PRECISION)
        polynomial_update = COEF_A * identity + COEF_B * gram_matrix + COEF_C * square
        current_weights = jnp.einsum(
            "hmrf,hmfg->hmrg", current_weights, polynomial_update, precision=FULL_PRECISION
        )
    return current_weights


def local(queries, keys, values, rates, fast_init):
    weights = lax.all_gather(fast_init, "seq", axis=2, tiled=True)
    head_count = weights.shape[0]
    head_size = weights.shape[2]
    results = []
    for group_index in range(queries.shape[0]):
        query_flat, key_flat, value_flat, rate_rows = (
            lax.all_to_all(queries[group_index], "head", split_axis=1, concat_axis=0, tiled=True),
            lax.all_to_all(keys[group_index], "head", split_axis=1, concat_axis=0, tiled=True),
            lax.all_to_all(values[group_index], "head", split_axis=1, concat_axis=0, tiled=True),
            lax.all_to_all(rates[group_index], "head", split_axis=1, concat_axis=0, tiled=True),
        )
        row_count = query_flat.shape[0]
        query_rows = query_flat.reshape(row_count, head_count, head_size)
        key_rows = key_flat.reshape(row_count, head_count, head_size)
        value_rows = value_flat.reshape(row_count, head_count, head_size)
        low = weights.astype(jnp.bfloat16)
        gate_pre = jnp.einsum(
            "rhd,hdf->rhf", key_rows, low[:, 0], preferred_element_type=jnp.float32
        )
        up_proj = jnp.einsum(
            "rhd,hdf->rhf", key_rows, low[:, 1], preferred_element_type=jnp.float32
        )
        activated_hidden, slope_value = silu_parts(gate_pre)
        hidden = (activated_hidden * up_proj).astype(jnp.bfloat16)
        out_grad = (
            -(rate_rows.astype(jnp.float32)[:, :, None] * value_rows.astype(jnp.float32))
        ).astype(jnp.bfloat16)
        hidden_grad = jnp.einsum(
            "rhd,hdf->rhf", out_grad, low[:, 2], preferred_element_type=jnp.float32
        )
        gate_grad = (hidden_grad * up_proj * slope_value).astype(jnp.bfloat16)
        up_grad = (hidden_grad * activated_hidden).astype(jnp.bfloat16)
        gradients = jnp.stack(
            [
                jnp.einsum("rhd,rhf->hdf", key_rows, gate_grad, preferred_element_type=jnp.float32),
                jnp.einsum("rhd,rhf->hdf", key_rows, up_grad, preferred_element_type=jnp.float32),
                jnp.einsum("rhd,rhf->hdf", out_grad, hidden, preferred_element_type=jnp.float32),
            ],
            axis=1,
        )
        total_grad = lax.psum(gradients, "seq")
        update = newton_schulz(total_grad, local_gram)
        weights = weights - LEARNING_STEP * update
        low = weights.astype(jnp.bfloat16)
        query_gate = jnp.einsum(
            "rhd,hdf->rhf", query_rows, low[:, 0], preferred_element_type=jnp.float32
        )
        query_up = jnp.einsum(
            "rhd,hdf->rhf", query_rows, low[:, 1], preferred_element_type=jnp.float32
        )
        query_act, unused_slope = silu_parts(query_gate)
        query_hidden = (query_act * query_up).astype(jnp.bfloat16)
        result = jnp.einsum(
            "rhf,hdf->rhd", query_hidden, low[:, 2], preferred_element_type=jnp.float32
        )
        results.append(result.astype(jnp.bfloat16).reshape(row_count, head_count * head_size))
    return jnp.stack(results)


def solution(mesh):
    return jax.shard_map(
        local,
        mesh=mesh,
        in_specs=(
            P(None, ("seq", "head"), None),
            P(None, ("seq", "head"), None),
            P(None, ("seq", "head"), None),
            P(None, ("seq", "head"), None),
            P("head", None, "seq", None),
        ),
        out_specs=P(None, "seq", "head"),
        check_vma=False,
    )
```

profile of v0, /device:TPU:0, one launch (start us, length us, event | category | flops | bytes accessed | tf_op | source)
XLA Modules:
  0.0 496.7 jit_solution(14485534307048518920)
XLA Ops:
  9.7 4.3 all-to-all-start
  17.7 3.5 all-to-all-start.2
  22.2 4.1 all-to-all-done.2
  30.1 4.8 all-to-all-done.1
  35.5 38.2 %all-gather.2.cloned.1.call-done = f32[4,3,512,256]{3,2,0,1:T(8,128)} async-done(((f32[4,3,32,256]{3,2,0,1:T(8,128)}), f32[4,3,512,256]{3,2,0,1:T(8,128)}) %all-gather.2.cloned.1.call-update) | async-done | bytes 6291472 | tf_op jit(solution)/shard_map/all_gather | solution.py:41
  89.5 3.4 all-to-all-start.5
  93.0 5.1 %all-to-all-done.5 = bf16[32,2,2048]{2,0,1:T(8,128)(2,1)S(1)} async-done(((bf16[32,2,2048]{2,0,1:T(8,128)(2,1)}), bf16[32,2,2048]{2,0,1:T(8,128)(2,1)S(1)}, u32[]{:S(2)}, u32[]{:S(2)}) %all-to-all-start.5) | async-done | bytes 262176 | tf_op jit(solution)/shard_map/all_to_all | solution.py:49
  102.2 4.5 all-to-all-done.6
  108.5 112.3 %all-reduce.3.cloned.1.call-done = f32[4,3,512,256]{2,3,0,1:T(8,128)} async-done(((f32[4,3,512,256]{2,3,0,1:T(8,128)}), f32[4,3,512,256]{2,3,0,1:T(8,128)}) %all-reduce.3.cloned.1.call-update) | async-done | bytes 6291472 | tf_op jit(solution)/shard_map/psum | solution.py:81
  220.8 19.0 %select_reduce_fusion.1 = (f32[4,3]{1,0:T(4,128)S(1)}, f32[4,3,256,256]{3,2,1,0:T(8,128)}) fusion(pred[256,256]{1,0:T(8,128)(4,1)S(1)} %iota_compare_fusion, f32[4,3,512,256]{2,3,0,1:T(8,128)} %all-reduce.3.cloned.1.call-done), kind=kOutput, calls=%fused_computation.31 | convolution fusion | flops 4833411072 | bytes 9502768 | tf_op jit(solution)/shard_map/hmrf,hmrg->hmfg/dot_general | solution.py:20
  239.9 6.4 %fusion.36 = f32[4,3,256,256]{3,2,1,0:T(8,128)S(1)} fusion(f32[4,3,256,256]{3,2,1,0:T(8,128)} %get-tuple-element.18, f32[4,3]{1,0:T(4,128)S(1)} %get-tuple-element.15), kind=kOutput, calls=%fused_computation.46 | convolution fusion | flops 2416705536 | bytes 6291504 | tf_op jit(solution)/shard_map/hmfg,hmgk->hmfk/dot_general | solution.py:32
  246.4 10.8 %fusion.2 = f32[4,3,512,256]{3,2,1,0:T(8,128)S(1)} fusion(f32[4,3,256,256]{3,2,1,0:T(8,128)S(1)} %fusion.36, f32[256,256]{1,0:T(8,128)S(1)} %broadcast_select_fusion, f32[4,3,256,256]{3,2,1,0:T(8,128)S(1)} %copy-done.1, f32[4,3]{1,0:T(4,128)S(1)} %get-tuple-element.15, f32[4,3,512,256]{2,3,0,1:T(8,128)S(1)} %bitcast.117, f32[4,3]{0,1:T(4,128)S(1)} %copy.76), kind=kOutput, calls=%fused_computation.4 | convolution fusion | flops 4837343232 | bytes 19136608 | tf_op jit(solution)/shard_map/hmrf,hmfg->hmrg/dot_general | solution.py:34
  257.2 10.6 %fusion.101 = f32[4,3,256,256]{3,2,1,0:T(8,128)S(1)} fusion(f32[4,3,512,256]{3,2,1,0:T(8,128)S(1)} %fusion.2), kind=kOutput, calls=%fused_computation.145 | convolution fusion | flops 4831838208 | bytes 9437184 | tf_op jit(solution)/shard_map/hmrf,hmrg->hmfg/dot_general | solution.py:20
  267.9 3.9 multiply_add_fusion.1
  271.8 8.1 %fusion.100 = (bf16[4,3,512,256]{3,2,0,1:T(8,128)(2,1)S(1)}, f32[4,3,512,256]{3,2,0,1:T(8,128)}) fusion(f32[4,3,512,256]{3,2,0,1:T(8,128)S(1)} %bitcast.115, f32[4,3,256,256]{3,2,1,0:T(8,128)S(1)} %multiply_add_fusion.1, f32[4,3,512,256]{3,2,1,0:T(8,128)S(1)} %fusion.2), kind=kOutput, calls=%fused_computation.144 | convolution fusion | flops 4836556800 | bytes 25165824 | tf_op jit(solution)/shard_map/hmrf,hmfg->hmrg/dot_general | solution.py:34
  291.5 4.1 all-to-all-start.3
  300.9 4.1 all-to-all-start.7
  318.4 107.0 %all-reduce.5.cloned.1.call-done = f32[4,3,512,256]{2,3,0,1:T(8,128)} async-done(((f32[4,3,512,256]{2,3,0,1:T(8,128)}), f32[4,3,512,256]{2,3,0,1:T(8,128)}) %all-reduce.5.cloned.1.call-update) | async-done | bytes 6291472 | tf_op jit(solution)/shard_map/psum | solution.py:81
  425.5 18.8 %select_reduce_fusion = (f32[4,3]{1,0:T(4,128)S(1)}, f32[4,3,256,256]{3,2,1,0:T(8,128)}) fusion(pred[256,256]{1,0:T(8,128)(4,1)S(1)} %iota_compare_fusion, f32[4,3,512,256]{2,3,0,1:T(8,128)} %all-reduce.5.cloned.1.call-done), kind=kOutput, calls=%fused_computation.24 | convolution fusion | flops 4833411072 | bytes 9502768 | tf_op jit(solution)/shard_map/hmrf,hmrg->hmfg/dot_general | solution.py:20
  444.4 6.7 %fusion.37 = f32[4,3,256,256]{3,2,1,0:T(8,128)S(1)} fusion(f32[4,3,256,256]{3,2,1,0:T(8,128)} %get-tuple-element.22, f32[4,3]{1,0:T(4,128)S(1)} %get-tuple-element.13), kind=kOutput, calls=%fused_computation.47 | convolution fusion | flops 2416705536 | bytes 6291504 | tf_op jit(solution)/shard_map/hmfg,hmgk->hmfk/dot_general | solution.py:32
  451.1 11.4 %fusion = f32[4,3,512,256]{3,2,1,0:T(8,128)S(1)} fusion(f32[4,3,256,256]{3,2,1,0:T(8,128)S(1)} %fusion.37, f32[256,256]{1,0:T(8,128)S(1)} %broadcast_select_fusion, f32[4,3,256,256]{3,2,1,0:T(8,128)S(1)} %copy-done, f32[4,3]{1,0:T(4,128)S(1)} %get-tuple-element.13, f32[4,3,512,256]{2,3,0,1:T(8,128)S(1)} %bitcast.119, f32[4,3]{0,1:T(4,128)S(1)} %copy.97), kind=kOutput, calls=%fused_computation.2 | convolution fusion | flops 4837343232 | bytes 19136608 | tf_op jit(solution)/shard_map/hmrf,hmfg->hmrg/dot_general | solution.py:34
  462.6 10.8 %fusion.102 = f32[4,3,256,256]{3,2,1,0:T(8,128)S(1)} fusion(f32[4,3,512,256]{3,2,1,0:T(8,128)S(1)} %fusion), kind=kOutput, calls=%fused_computation.146 | convolution fusion | flops 4831838208 | bytes 9437184 | tf_op jit(solution)/shard_map/hmrf,hmrg->hmfg/dot_general | solution.py:20
  473.4 4.1 multiply_add_fusion
  477.6 6.5 %subtract_convert_fusion = bf16[4,3,512,256]{3,2,0,1:T(8,128)(2,1)S(1)} fusion(f32[4,3,512,256]{3,2,0,1:T(8,128)S(1)} %bitcast.113, f32[4,3,256,256]{3,2,1,0:T(8,128)S(1)} %multiply_add_fusion, f32[4,3,512,256]{3,2,1,0:T(8,128)S(1)} %fusion), kind=kOutput, calls=%fused_computation.14 | convolution fusion | flops 4836556800 | bytes 18874368 | tf_op jit(solution)/shard_map/hmrf,hmfg->hmrg/dot_general | solution.py:34
  (108 shorter events, 70.0 us)
Async XLA Ops:
  6.5 14.7 %copy-start.5 = (bf16[2,32,4096]{2,1,0:T(8,128)(2,1)S(1)}, bf16[2,32,4096]{2,1,0:T(8,128)(2,1)}, u32[]{:S(2)}) copy-start(bf16[2,32,4096]{2,1,0:T(8,128)(2,1)} %param.7) | copy-start | bytes 1572868
  6.5 67.2 %all-gather.2.cloned.1.call-start = ((), (), s32[]{:S(2)}) async-start(), calls=%async_computation.8 | async-start | bytes 6684672 | tf_op jit(solution)/shard_map/all_gather | solution.py:41
  9.7 8.0 %all-to-all-start = ((bf16[32,2,4]{0,2,1:T(4,128)(2,1)}), bf16[32,2,4]{0,2,1:T(4,128)(2,1)S(1)}, u32[]{:S(2)}, u32[]{:S(2)}) async-start(bf16[32,2,4]{0,2,1:T(4,128)(2,1)} %bitcast), calls=%async_computation | async-start | bytes 4096 | tf_op jit(solution)/shard_map/all_to_all | solution.py:50
  17.7 8.6 %all-to-all-start.2 = ((bf16[32,2,2048]{2,0,1:T(8,128)(2,1)}), bf16[32,2,2048]{2,0,1:T(8,128)(2,1)S(1)}, u32[]{:S(2)}, u32[]{:S(2)}) async-start(bf16[32,2,2048]{2,0,1:T(8,128)(2,1)} %copy.67), calls=%async_computation.2 | async-start | bytes 524288 | tf_op jit(solution)/shard_map/all_to_all | solution.py:48
  26.4 8.6 %all-to-all-start.1 = ((bf16[32,2,2048]{2,0,1:T(8,128)(2,1)}), bf16[32,2,2048]{2,0,1:T(8,128)(2,1)S(1)}, u32[]{:S(2)}, u32[]{:S(2)}) async-start(bf16[32,2,2048]{2,0,1:T(8,128)(2,1)} %copy.65), calls=%async_computation.1 | async-start | bytes 524288 | tf_op jit(solution)/shard_map/all_to_all | solution.py:49
  29.8 191.0 %all-reduce.3.cloned.1.call-start = ((), (), s32[]{:S(2)}) async-start(), calls=%async_computation.9 | async-start | bytes 12582912 | tf_op jit(solution)/shard_map/psum | solution.py:81
  82.6 6.8 %all-to-all-start.4 = ((bf16[32,2,4]{0,2,1:T(4,128)(2,1)}), bf16[32,2,4]{0,2,1:T(4,128)(2,1)S(1)}, u32[]{:S(2)}, u32[]{:S(2)}) async-start(bf16[32,2,4]{0,2,1:T(4,128)(2,1)} %bitcast.23), calls=%async_computation.4 | async-start | bytes 4096 | tf_op jit(solution)/shard_map/all_to_all | solution.py:50
  89.5 8.6 %all-to-all-start.5 = ((bf16[32,2,2048]{2,0,1:T(8,128)(2,1)}), bf16[32,2,2048]{2,0,1:T(8,128)(2,1)S(1)}, u32[]{:S(2)}, u32[]{:S(2)}) async-start(bf16[32,2,2048]{2,0,1:T(8,128)(2,1)} %copy.86), calls=%async_computation.5 | async-start | bytes 524288 | tf_op jit(solution)/shard_map/all_to_all | solution.py:49
  98.1 8.6 %all-to-all-start.6 = ((bf16[32,2,2048]{2,0,1:T(8,128)(2,1)}), bf16[32,2,2048]{2,0,1:T(8,128)(2,1)S(1)}, u32[]{:S(2)}, u32[]{:S(2)}) async-start(bf16[32,2,2048]{2,0,1:T(8,128)(2,1)} %copy.88), calls=%async_computation.6 | async-start | bytes 524288 | tf_op jit(solution)/shard_map/all_to_all | solution.py:48
  101.5 324.0 %all-reduce.5.cloned.1.call-start = ((), (), s32[]{:S(2)}) async-start(), calls=%async_computation.10 | async-start | bytes 12582912 | tf_op jit(solution)/shard_map/psum | solution.py:81
  220.8 25.5 %slice-start.4 = ((s8[6291456]{0:T(1024)(128)(4,1)}), s8[2097152]{0:T(1024)(128)(4,1)S(1)}, s32[]{:S(2)}) async-start(s8[6291456]{0:T(1024)(128)(4,1)} %bitcast.116), calls=%async_computation.15 | async-start | bytes 4194304
  239.9 6.4 %slice-start.5 = ((s8[6291456]{0:T(1024)(128)(4,1)}), s8[4194304]{0:T(1024)(128)(4,1)S(1)}, s32[]{:S(2)}) async-start(s8[6291456]{0:T(1024)(128)(4,1)} %bitcast.116), calls=%async_computation.16 | async-start | bytes 8388608
  239.9 6.4 %copy-start.1 = (f32[4,3,256,256]{3,2,1,0:T(8,128)S(1)}, f32[4,3,256,256]{3,2,1,0:T(8,128)}, u32[]{:S(2)}) copy-start(f32[4,3,256,256]{3,2,1,0:T(8,128)} %get-tuple-element.18) | copy-start | bytes 9437188
  239.9 31.8 %slice-start.2 = ((s8[6291456]{0:T(1024)(128)(4,1)}), s8[4194304]{0:T(1024)(128)(4,1)S(1)}, s32[]{:S(2)}) async-start(s8[6291456]{0:T(1024)(128)(4,1)} %bitcast.114), calls=%async_computation.13 | async-start | bytes 8388608
  246.4 25.4 %slice-start.3 = ((s8[6291456]{0:T(1024)(128)(4,1)}), s8[2097152]{0:T(1024)(128)(4,1)S(1)}, s32[]{:S(2)}) async-start(s8[6291456]{0:T(1024)(128)(4,1)} %bitcast.114), calls=%async_computation.14 | async-start | bytes 4194304
  271.8 8.1 %copy-start.2 = (bf16[64,4,512]{2,1,0:T(4,128)(2,1)S(1)}, bf16[64,4,512]{2,1,0:T(4,128)(2,1)}, u32[]{:S(2)}) copy-start(bf16[64,4,512]{2,1,0:T(4,128)(2,1)} %reshape.94) | copy-start | bytes 786436
  291.5 9.4 %all-to-all-start.3 = ((bf16[32,2,2048]{2,0,1:T(8,128)(2,1)}), bf16[32,2,2048]{2,0,1:T(8,128)(2,1)}, u32[]{:S(2)}, u32[]{:S(2)}) async-start(bf16[32,2,2048]{2,0,1:T(8,128)(2,1)} %copy.80), calls=%async_computation.3 | async-start | bytes 524288 | tf_op jit(solution)/shard_map/all_to_all | solution.py:47
  300.9 9.4 %all-to-all-start.7 = ((bf16[32,2,2048]{2,0,1:T(8,128)(2,1)}), bf16[32,2,2048]{2,0,1:T(8,128)(2,1)}, u32[]{:S(2)}, u32[]{:S(2)}) async-start(bf16[32,2,2048]{2,0,1:T(8,128)(2,1)} %copy.101), calls=%async_computation.7 | async-start | bytes 524288 | tf_op jit(solution)/shard_map/all_to_all | solution.py:47
  425.5 25.6 %slice-start.6 = ((s8[6291456]{0:T(1024)(128)(4,1)}), s8[2097152]{0:T(1024)(128)(4,1)S(1)}, s32[]{:S(2)}) async-start(s8[6291456]{0:T(1024)(128)(4,1)} %bitcast.118), calls=%async_computation.17 | async-start | bytes 4194304
  444.4 6.7 %slice-start.7 = ((s8[6291456]{0:T(1024)(128)(4,1)}), s8[4194304]{0:T(1024)(128)(4,1)S(1)}, s32[]{:S(2)}) async-start(s8[6291456]{0:T(1024)(128)(4,1)} %bitcast.118), calls=%async_computation.18 | async-start | bytes 8388608
  444.4 6.7 %copy-start = (f32[4,3,256,256]{3,2,1,0:T(8,128)S(1)}, f32[4,3,256,256]{3,2,1,0:T(8,128)}, u32[]{:S(2)}) copy-start(f32[4,3,256,256]{3,2,1,0:T(8,128)} %get-tuple-element.22) | copy-start | bytes 9437188
  444.4 33.2 %slice-start = ((s8[6291456]{0:T(1024)(128)(4,1)}), s8[4194304]{0:T(1024)(128)(4,1)S(1)}, s32[]{:S(2)}) async-start(s8[6291456]{0:T(1024)(128)(4,1)} %bitcast.112), calls=%async_computation.11 | async-start | bytes 8388608
  451.1 26.4 %slice-start.1 = ((s8[6291456]{0:T(1024)(128)(4,1)}), s8[2097152]{0:T(1024)(128)(4,1)S(1)}, s32[]{:S(2)}) async-start(s8[6291456]{0:T(1024)(128)(4,1)} %bitcast.112), calls=%async_computation.12 | async-start | bytes 4194304
  477.6 6.6 %copy-start.6 = (bf16[64,4,512]{2,1,0:T(4,128)(2,1)S(1)}, bf16[64,4,512]{2,1,0:T(4,128)(2,1)}, u32[]{:S(2)}) copy-start(bf16[64,4,512]{2,1,0:T(4,128)(2,1)} %reshape.95) | copy-start | bytes 786436
  (2 other events, 5.7 us)
Sparse Core Ops, SparseCore 0:
  9.5 64.1 all-gather.1
  82.7 137.9 all-reduce.2
  286.1 139.3 all-reduce.4
where the time goes:
time: 502 us; the launch traced here: 497 us
  waiting for transfers between devices  285 us (57%)
  matrix products  130 us (26%)
  starting transfers between devices  29.8 us (6%)
  local copies, waits for them, and re-layouts  26.7 us (5%)
  between operations  14.1 us (3%)
  other arithmetic  11.8 us (2%)
    psum x2, waiting for transfers between devices, local(): total_grad = lax.psum(gradients, 'seq')  219 us
    dot_general x4, matrix products, local_gram(): jnp.einsum('hmrf,hmrg->hmfg', weight_matrices, weight_matrices, precision...  59.2 us
    all_gather x1, waiting for transfers between devices, local(): weights = lax.all_gather(fast_init, 'seq', axis=2, tiled=True)  38.2 us
    dot_general x4, matrix products, newton_schulz(): jnp.einsum('hmrf,hmfg->hmrg', current_weights, polynomial_update, precisi...  36.9 us
    dot_general x4, matrix products, newton_schulz(): jnp.einsum('hmfg,hmgk->hmfk', gram_matrix, gram_matrix, precision=FULL_PR...  21.1 us
  transfers between devices with their start and end apart: 11, of which 11 were waited for; matrix products, arithmetic and copies ran while one was open for 5% of the time, Pallas kernels for 0%

commit v1 on v0

--- a/solution.py
+++ b/solution.py
@@ -9,6 +9,31 @@
 COEF_C = 2.0315
 LEARNING_STEP = 0.5
 FULL_PRECISION = lax.Precision.HIGHEST
+
+
+def measure_counts(sample, dev_axis, in_dim):
+    last = jax.lax.axis_size(dev_axis)
+    built = jax.lax.axis_index(dev_axis)
+    v_now, clean, front = (last, built, sample.shape[in_dim])
+    made = [it * v_now if jj == in_dim else it for jj, it in enumerate(sample.shape)]
+    local_now = jnp.zeros(made, sample.dtype)
+    state_now = lax.dynamic_update_slice_in_dim(local_now, sample, clean * front, axis=in_dim)
+    response = field_out = sample
+    for ix in range(1, v_now // 2 + 1):
+        response = jax.lax.ppermute(
+            response, dev_axis, [(jj, (jj + 1) % v_now) for jj in range(v_now)]
+        )
+        state_now = lax.dynamic_update_slice_in_dim(
+            state_now, response, (clean - ix) % v_now * front, axis=in_dim
+        )
+        if 2 * ix < v_now:
+            field_out = jax.lax.ppermute(
+                field_out, dev_axis, [(jj, (jj - 1) % v_now) for jj in range(v_now)]
+            )
+            state_now = lax.dynamic_update_slice_in_dim(
+                state_now, field_out, (clean + ix) % v_now * front, axis=in_dim
+            )
+    return state_now
 
 
 def silu_parts(gate_pre):
@@ -38,7 +63,7 @@
 
 
 def local(queries, keys, values, rates, fast_init):
-    weights = lax.all_gather(fast_init, "seq", axis=2, tiled=True)
+    weights = measure_counts(fast_init, "seq", 2)
     head_count = weights.shape[0]
     head_size = weights.shape[2]
     results = []

time: 502 us -> 537 us (1.070)
  starting transfers between devices: 29.8 us -> 64 us
  waiting for transfers between devices: 285 us -> 264 us
  local copies, waits for them, and re-layouts: 26.7 us -> 44.1 us
    all_gather x1 -> x0, waiting for transfers between devices: 38.2 us -> none  [local(): weights = lax.all_gather(fast_init, 'seq', axis=2, tiled=True)]
    ppermute x0 -> x15, starting transfers between devices: none -> 35.3 us  [the longest x7 29.2 us: measure_counts(): jax.lax.ppermute(field_out, dev_axis, [(jj, (jj - 1) % v_now) for jj in r...]
    ppermute x0 -> x15, waiting for transfers between devices: none -> 18.6 us  [the longest x8 16.8 us: measure_counts(): jax.lax.ppermute(response, dev_axis, [(jj, (jj + 1) % v_now) for jj in ra...]
    dynamic_update_slice x0 -> x15, local copies, waits for them, and re-layouts: none -> 16.8 us  [the longest x7 8.5 us: measure_counts(): lax.dynamic_update_slice_in_dim(state_now, field_out, (clean + ix) % v_no...]
  transfers between devices with their start and end apart: 11 -> 25, of which waited for: 11 -> 14; matrix products, arithmetic and copies ran while one was open for 5% -> 7% of each run, Pallas kernels for 0% -> 0%
where the time goes in v1:
time: 537 us; the launch traced here: 530 us
  waiting for transfers between devices  264 us (49%)
  matrix products  132 us (25%)
  starting transfers between devices  64 us (12%)
  local copies, waits for them, and re-layouts  44.1 us (8%)
  between operations  14.6 us (3%)
  other arithmetic  11.9 us (2%)
    psum x2, waiting for transfers between devices, local(): total_grad = lax.psum(gradients, 'seq')  224 us
    dot_general x4, matrix products, local_gram(): jnp.einsum('hmrf,hmrg->hmfg', weight_matrices, weight_matrices, precision...  59.2 us
    dot_general x4, matrix products, newton_schulz(): jnp.einsum('hmrf,hmfg->hmrg', current_weights, polynomial_update, precisi...  38.8 us
    ppermute x7, starting transfers between devices, measure_counts(): jax.lax.ppermute(field_out, dev_axis, [(jj, (jj - 1) % v_now) for jj in r...  29.2 us
    dot_general x4, matrix products, newton_schulz(): jnp.einsum('hmfg,hmgk->hmfk', gram_matrix, gram_matrix, precision=FULL_PR...  21.1 us
    ppermute x8, waiting for transfers between devices, measure_counts(): jax.lax.ppermute(response, dev_axis, [(jj, (jj + 1) % v_now) for jj in ra...  16.8 us
  transfers between devices with their start and end apart: 25, of which 14 were waited for; matrix products, arithmetic and copies ran while one was open for 7% of the time, Pallas kernels for 0%

profile of v1, /device:TPU:0, one launch (start us, length us, event | category | flops | bytes accessed | tf_op | source)
XLA Modules:
  0.0 530.0 jit_solution(6141894584587948797)
XLA Ops:
  11.2 4.9 collective-permute-start.1
  26.1 5.5 %collective-permute-done.2 = f32[4,3,32,256]{3,2,0,1:T(8,128)S(1)} collective-permute-done((f32[4,3,32,256]{3,2,0,1:T(8,128)S(1)}, f32[4,3,32,256]{3,2,0,1:T(8,128)S(1)}, u32[]{:S(2)}, u32[]{:S(2)}) %collective-permute-start.2) | collective-permute-done | bytes 393248 | tf_op jit(solution)/shard_map/ppermute | solution.py:23
  44.4 4.3 collective-permute-start.7
  52.7 4.7 all-to-all-done.2
  58.6 5.1 collective-permute-start.9
  72.8 4.5 collective-permute-start.11
  83.4 4.4 collective-permute-start.13
  93.9 5.2 collective-permute-done.14
  119.5 5.1 all-to-all-done.5
  128.7 4.5 all-to-all-done.6
  134.9 117.1 %all-reduce.3.cloned.1.call-done = f32[4,3,512,256]{2,3,0,1:T(8,128)} async-done(((f32[4,3,512,256]{2,3,0,1:T(8,128)}), f32[4,3,512,256]{2,3,0,1:T(8,128)}) %all-reduce.3.cloned.1.call-update) | async-done | bytes 6291472 | tf_op jit(solution)/shard_map/psum | solution.py:106
  252.0 19.0 %select_reduce_fusion.1 = (f32[4,3]{1,0:T(4,128)S(1)}, f32[4,3,256,256]{3,2,1,0:T(8,128)}) fusion(pred[256,256]{1,0:T(8,128)(4,1)S(1)} %iota_compare_fusion, f32[4,3,512,256]{2,3,0,1:T(8,128)} %all-reduce.3.cloned.1.call-done), kind=kOutput, calls=%fused_computation.31 | convolution fusion | flops 4833411072 | bytes 9502768 | tf_op jit(solution)/shard_map/hmrf,hmrg->hmfg/dot_general | solution.py:45
  271.1 6.4 %fusion.36 = f32[4,3,256,256]{3,2,1,0:T(8,128)S(1)} fusion(f32[4,3,256,256]{3,2,1,0:T(8,128)} %get-tuple-element.20, f32[4,3]{1,0:T(4,128)S(1)} %get-tuple-element.17), kind=kOutput, calls=%fused_computation.46 | convolution fusion | flops 2416705536 | bytes 6291504 | tf_op jit(solution)/shard_map/hmfg,hmgk->hmfk/dot_general | solution.py:57
  277.6 10.8 %fusion.2 = f32[4,3,512,256]{3,2,1,0:T(8,128)S(1)} fusion(f32[4,3,256,256]{3,2,1,0:T(8,128)S(1)} %fusion.36, f32[256,256]{1,0:T(8,128)S(1)} %broadcast_select_fusion, f32[4,3,256,256]{3,2,1,0:T(8,128)S(1)} %copy-done.1, f32[4,3]{1,0:T(4,128)S(1)} %get-tuple-element.17, f32[4,3,512,256]{2,3,0,1:T(8,128)S(1)} %bitcast.115, f32[4,3]{0,1:T(4,128)S(1)} %copy.82), kind=kOutput, calls=%fused_computation.4 | convolution fusion | flops 4837343232 | bytes 19136608 | tf_op jit(solution)/shard_map/hmrf,hmfg->hmrg/dot_general | solution.py:59
  288.4 10.6 %fusion.102 = f32[4,3,256,256]{3,2,1,0:T(8,128)S(1)} fusion(f32[4,3,512,256]{3,2,1,0:T(8,128)S(1)} %fusion.2), kind=kOutput, calls=%fused_computation.162 | convolution fusion | flops 4831838208 | bytes 9437184 | tf_op jit(solution)/shard_map/hmrf,hmrg->hmfg/dot_general | solution.py:45
  302.9 10.0 %fusion.101 = (bf16[4,3,512,256]{3,2,0,1:T(8,128)(2,1)S(1)}, f32[4,3,512,256]{3,2,0,1:T(8,128)}) fusion(f32[4,3,512,256]{3,2,0,1:T(8,128)} %constant_dynamic-update-slice_fusion, f32[4,3,256,256]{3,2,1,0:T(8,128)S(1)} %multiply_add_fusion.1, f32[4,3,512,256]{3,2,1,0:T(8,128)S(1)} %fusion.2), kind=kOutput, calls=%fused_computation.161 | convolution fusion | flops 4836556800 | bytes 25165824 | tf_op jit(solution)/shard_map/hmrf,hmfg->hmrg/dot_general | solution.py:59
  324.5 4.1 all-to-all-start.3
  351.5 107.0 %all-reduce.5.cloned.1.call-done = f32[4,3,512,256]{2,3,0,1:T(8,128)} async-done(((f32[4,3,512,256]{2,3,0,1:T(8,128)}), f32[4,3,512,256]{2,3,0,1:T(8,128)}) %all-reduce.5.cloned.1.call-update) | async-done | bytes 6291472 | tf_op jit(solution)/shard_map/psum | solution.py:106
  458.6 18.7 %select_reduce_fusion = (f32[4,3]{1,0:T(4,128)S(1)}, f32[4,3,256,256]{3,2,1,0:T(8,128)}) fusion(pred[256,256]{1,0:T(8,128)(4,1)S(1)} %iota_compare_fusion, f32[4,3,512,256]{2,3,0,1:T(8,128)} %all-reduce.5.cloned.1.call-done), kind=kOutput, calls=%fused_computation.24 | convolution fusion | flops 4833411072 | bytes 9502768 | tf_op jit(solution)/shard_map/hmrf,hmrg->hmfg/dot_general | solution.py:45
  477.4 6.7 %fusion.37 = f32[4,3,256,256]{3,2,1,0:T(8,128)S(1)} fusion(f32[4,3,256,256]{3,2,1,0:T(8,128)} %get-tuple-element.24, f32[4,3]{1,0:T(4,128)S(1)} %get-tuple-element.15), kind=kOutput, calls=%fused_computation.47 | convolution fusion | flops 2416705536 | bytes 6291504 | tf_op jit(solution)/shard_map/hmfg,hmgk->hmfk/dot_general | solution.py:57
  484.2 11.4 %fusion = f32[4,3,512,256]{3,2,1,0:T(8,128)S(1)} fusion(f32[4,3,256,256]{3,2,1,0:T(8,128)S(1)} %fusion.37, f32[256,256]{1,0:T(8,128)S(1)} %broadcast_select_fusion, f32[4,3,256,256]{3,2,1,0:T(8,128)S(1)} %copy-done, f32[4,3]{1,0:T(4,128)S(1)} %get-tuple-element.15, f32[4,3,512,256]{2,3,0,1:T(8,128)S(1)} %bitcast.117, f32[4,3]{0,1:T(4,128)S(1)} %copy.103), kind=kOutput, calls=%fused_computation.2 | convolution fusion | flops 4837343232 | bytes 19136608 | tf_op jit(solution)/shard_map/hmrf,hmfg->hmrg/dot_general | solution.py:59
  495.6 10.8 %fusion.103 = f32[4,3,256,256]{3,2,1,0:T(8,128)S(1)} fusion(f32[4,3,512,256]{3,2,1,0:T(8,128)S(1)} %fusion), kind=kOutput, calls=%fused_computation.163 | convolution fusion | flops 4831838208 | bytes 9437184 | tf_op jit(solution)/shard_map/hmrf,hmrg->hmfg/dot_general | solution.py:45
  506.5 4.1 multiply_add_fusion
  510.6 6.5 %subtract_convert_fusion = bf16[4,3,512,256]{3,2,0,1:T(8,128)(2,1)S(1)} fusion(f32[4,3,512,256]{3,2,0,1:T(8,128)S(1)} %bitcast.113, f32[4,3,256,256]{3,2,1,0:T(8,128)S(1)} %multiply_add_fusion, f32[4,3,512,256]{3,2,1,0:T(8,128)S(1)} %fusion), kind=kOutput, calls=%fused_computation.14 | convolution fusion | flops 4836556800 | bytes 18874368 | tf_op jit(solution)/shard_map/hmrf,hmfg->hmrg/dot_general | solution.py:59
  (152 shorter events, 123.7 us)
Async XLA Ops:
  10.6 11.0 %collective-permute-start = (f32[4,3,32,256]{3,2,0,1:T(8,128)S(1)}, f32[4,3,32,256]{3,2,0,1:T(8,128)S(1)}, u32[]{:S(2)}, u32[]{:S(2)}) collective-permute-start(f32[4,3,32,256]{3,2,0,1:T(8,128)S(1)} %get-tuple-element.11), channel_id=1, source_target_pairs={{0,2},{2,4},{4,6},{6,8},{8,10},{10,12},{12,14},{14,16},{16,18},{18... | collective-permute-start | bytes 1179656 | tf_op jit(solution)/shard_map/ppermute | solution.py:23
  11.2 11.5 %collective-permute-start.1 = (f32[4,3,32,256]{3,2,0,1:T(8,128)S(1)}, f32[4,3,32,256]{3,2,0,1:T(8,128)S(1)}, u32[]{:S(2)}, u32[]{:S(2)}) collective-permute-start(f32[4,3,32,256]{3,2,0,1:T(8,128)S(1)} %get-tuple-element.11), channel_id=1, source_target_pairs={{0,30},{2,0},{4,2},{6,4},{8,6},{10,8},{12,10},{14,12},{16,14},{18,... | collective-permute-start | bytes 1179656 | tf_op jit(solution)/shard_map/ppermute | solution.py:30
  16.6 21.8 %all-to-all-start = ((bf16[32,2,4]{0,2,1:T(4,128)(2,1)}), bf16[32,2,4]{0,2,1:T(4,128)(2,1)S(1)}, u32[]{:S(2)}, u32[]{:S(2)}) async-start(bf16[32,2,4]{0,2,1:T(4,128)(2,1)} %bitcast.1), calls=%async_computation | async-start | bytes 4096 | tf_op jit(solution)/shard_map/all_to_all | solution.py:75
  21.6 10.0 %collective-permute-start.2 = (f32[4,3,32,256]{3,2,0,1:T(8,128)S(1)}, f32[4,3,32,256]{3,2,0,1:T(8,128)S(1)}, u32[]{:S(2)}, u32[]{:S(2)}) collective-permute-start(f32[4,3,32,256]{3,2,0,1:T(8,128)S(1)} %collective-permute-done), channel_id=1, source_target_pairs={{0,2},{2,4},{4,6},{6,8},{8,10},{10,12},{12,14},{14,16},{16,18},{18... | collective-permute-start | bytes 1179656 | tf_op jit(solution)/shard_map/ppermute | solution.py:23
  22.6 10.9 %collective-permute-start.3 = (f32[4,3,32,256]{3,2,0,1:T(8,128)S(1)}, f32[4,3,32,256]{3,2,0,1:T(8,128)}, u32[]{:S(2)}, u32[]{:S(2)}) collective-permute-start(f32[4,3,32,256]{3,2,0,1:T(8,128)S(1)} %collective-permute-done.1), channel_id=1, source_target_pairs={{0,30},{2,0},{4,2},{6,4},{8,6},{10,8},{12,10},{14,12},{16,14},{18,... | collective-permute-start | bytes 1179656 | tf_op jit(solution)/shard_map/ppermute | solution.py:30
  31.6 10.4 %collective-permute-start.4 = (f32[4,3,32,256]{3,2,0,1:T(8,128)S(1)}, f32[4,3,32,256]{3,2,0,1:T(8,128)}, u32[]{:S(2)}, u32[]{:S(2)}) collective-permute-start(f32[4,3,32,256]{3,2,0,1:T(8,128)S(1)} %collective-permute-done.2), channel_id=1, source_target_pairs={{0,2},{2,4},{4,6},{6,8},{8,10},{10,12},{12,14},{14,16},{16,18},{18... | collective-permute-start | bytes 1179656 | tf_op jit(solution)/shard_map/ppermute | solution.py:23
  33.6 10.8 %collective-permute-start.5 = (f32[4,3,32,256]{3,2,0,1:T(8,128)}, f32[4,3,32,256]{3,2,0,1:T(8,128)}, u32[]{:S(2)}, u32[]{:S(2)}) collective-permute-start(f32[4,3,32,256]{3,2,0,1:T(8,128)} %collective-permute-done.3), channel_id=1, source_target_pairs={{0,30},{2,0},{4,2},{6,4},{8,6},{10,8},{12,10},{14,12},{16,14},{18,... | collective-permute-start | bytes 1179656 | tf_op jit(solution)/shard_map/ppermute | solution.py:30
  38.4 10.4 %all-to-all-start.1 = ((bf16[32,2,2048]{2,0,1:T(8,128)(2,1)}), bf16[32,2,2048]{2,0,1:T(8,128)(2,1)S(1)}, u32[]{:S(2)}, u32[]{:S(2)}) async-start(bf16[32,2,2048]{2,0,1:T(8,128)(2,1)} %copy.71), calls=%async_computation.1 | async-start | bytes 524288 | tf_op jit(solution)/shard_map/all_to_all | solution.py:74
  42.0 15.6 %collective-permute-start.6 = (f32[4,3,32,256]{3,2,0,1:T(8,128)}, f32[4,3,32,256]{3,2,0,1:T(8,128)}, u32[]{:S(2)}, u32[]{:S(2)}) collective-permute-start(f32[4,3,32,256]{3,2,0,1:T(8,128)} %collective-permute-done.4), channel_id=1, source_target_pairs={{0,2},{2,4},{4,6},{6,8},{8,10},{10,12},{12,14},{14,16},{16,18},{18... | collective-permute-start | bytes 1179656 | tf_op jit(solution)/shard_map/ppermute | solution.py:23
  44.4 14.2 %collective-permute-start.7 = (f32[4,3,32,256]{3,2,0,1:T(8,128)}, f32[4,3,32,256]{3,2,0,1:T(8,128)}, u32[]{:S(2)}, u32[]{:S(2)}) collective-permute-start(f32[4,3,32,256]{3,2,0,1:T(8,128)} %collective-permute-done.5), channel_id=1, source_target_pairs={{0,30},{2,0},{4,2},{6,4},{8,6},{10,8},{12,10},{14,12},{16,14},{18,... | collective-permute-start | bytes 1179656 | tf_op jit(solution)/shard_map/ppermute | solution.py:30
  48.8 8.6 %all-to-all-start.2 = ((bf16[32,2,2048]{2,0,1:T(8,128)(2,1)}), bf16[32,2,2048]{2,0,1:T(8,128)(2,1)S(1)}, u32[]{:S(2)}, u32[]{:S(2)}) async-start(bf16[32,2,2048]{2,0,1:T(8,128)(2,1)} %copy.73), calls=%async_computation.2 | async-start | bytes 524288 | tf_op jit(solution)/shard_map/all_to_all | solution.py:73
  52.2 199.8 %all-reduce.3.cloned.1.call-start = ((), (), s32[]{:S(2)}) async-start(), calls=%async_computation.8 | async-start | bytes 12582912 | tf_op jit(solution)/shard_map/psum | solution.py:106
  57.6 10.9 %collective-permute-start.8 = (f32[4,3,32,256]{3,2,0,1:T(8,128)}, f32[4,3,32,256]{3,2,0,1:T(8,128)S(1)}, u32[]{:S(2)}, u32[]{:S(2)}) collective-permute-start(f32[4,3,32,256]{3,2,0,1:T(8,128)} %collective-permute-done.6), channel_id=1, source_target_pairs={{0,2},{2,4},{4,6},{6,8},{8,10},{10,12},{12,14},{14,16},{16,18},{18... | collective-permute-start | bytes 1179656 | tf_op jit(solution)/shard_map/ppermute | solution.py:23
  58.6 14.2 %collective-permute-start.9 = (f32[4,3,32,256]{3,2,0,1:T(8,128)}, f32[4,3,32,256]{3,2,0,1:T(8,128)S(1)}, u32[]{:S(2)}, u32[]{:S(2)}) collective-permute-start(f32[4,3,32,256]{3,2,0,1:T(8,128)} %collective-permute-done.7), channel_id=1, source_target_pairs={{0,30},{2,0},{4,2},{6,4},{8,6},{10,8},{12,10},{14,12},{16,14},{18,... | collective-permute-start | bytes 1179656 | tf_op jit(solution)/shard_map/ppermute | solution.py:30
  68.4 10.6 %collective-permute-start.10 = (f32[4,3,32,256]{3,2,0,1:T(8,128)S(1)}, f32[4,3,32,256]{3,2,0,1:T(8,128)S(1)}, u32[]{:S(2)}, u32[]{:S(2)}) collective-permute-start(f32[4,3,32,256]{3,2,0,1:T(8,128)S(1)} %collective-permute-done.8), channel_id=1, source_target_pairs={{0,2},{2,4},{4,6},{6,8},{8,10},{10,12},{12,14},{14,16},{16,18},{18... | collective-permute-start | bytes 1179656 | tf_op jit(solution)/shard_map/ppermute | solution.py:23
  72.8 10.6 %collective-permute-start.11 = (f32[4,3,32,256]{3,2,0,1:T(8,128)S(1)}, f32[4,3,32,256]{3,2,0,1:T(8,128)S(1)}, u32[]{:S(2)}, u32[]{:S(2)}) collective-permute-start(f32[4,3,32,256]{3,2,0,1:T(8,128)S(1)} %collective-permute-done.9), channel_id=1, source_target_pairs={{0,30},{2,0},{4,2},{6,4},{8,6},{10,8},{12,10},{14,12},{16,14},{18,... | collective-permute-start | bytes 1179656 | tf_op jit(solution)/shard_map/ppermute | solution.py:30
  79.0 10.0 %collective-permute-start.12 = (f32[4,3,32,256]{3,2,0,1:T(8,128)S(1)}, f32[4,3,32,256]{3,2,0,1:T(8,128)S(1)}, u32[]{:S(2)}, u32[]{:S(2)}) collective-permute-start(f32[4,3,32,256]{3,2,0,1:T(8,128)S(1)} %collective-permute-done.10), channel_id=1, source_target_pairs={{0,2},{2,4},{4,6},{6,8},{8,10},{10,12},{12,14},{14,16},{16,18},{18... | collective-permute-start | bytes 1179656 | tf_op jit(solution)/shard_map/ppermute | solution.py:23
  83.4 9.7 %collective-permute-start.13 = (f32[4,3,32,256]{3,2,0,1:T(8,128)S(1)}, f32[4,3,32,256]{3,2,0,1:T(8,128)S(1)}, u32[]{:S(2)}, u32[]{:S(2)}) collective-permute-start(f32[4,3,32,256]{3,2,0,1:T(8,128)S(1)} %collective-permute-done.11), channel_id=1, source_target_pairs={{0,30},{2,0},{4,2},{6,4},{8,6},{10,8},{12,10},{14,12},{16,14},{18,... | collective-permute-start | bytes 1179656 | tf_op jit(solution)/shard_map/ppermute | solution.py:30
  89.0 10.1 %collective-permute-start.14 = (f32[4,3,32,256]{3,2,0,1:T(8,128)S(1)}, f32[4,3,32,256]{3,2,0,1:T(8,128)S(1)}, u32[]{:S(2)}, u32[]{:S(2)}) collective-permute-start(f32[4,3,32,256]{3,2,0,1:T(8,128)S(1)} %collective-permute-done.12), channel_id=1, source_target_pairs={{0,2},{2,4},{4,6},{6,8},{8,10},{10,12},{12,14},{14,16},{16,18},{18... | collective-permute-start | bytes 1179656 | tf_op jit(solution)/shard_map/ppermute | solution.py:23
  115.9 8.7 %all-to-all-start.5 = ((bf16[32,2,2048]{2,0,1:T(8,128)(2,1)}), bf16[32,2,2048]{2,0,1:T(8,128)(2,1)S(1)}, u32[]{:S(2)}, u32[]{:S(2)}) async-start(bf16[32,2,2048]{2,0,1:T(8,128)(2,1)} %copy.92), calls=%async_computation.5 | async-start | bytes 524288 | tf_op jit(solution)/shard_map/all_to_all | solution.py:74
  124.5 8.6 %all-to-all-start.6 = ((bf16[32,2,2048]{2,0,1:T(8,128)(2,1)}), bf16[32,2,2048]{2,0,1:T(8,128)(2,1)S(1)}, u32[]{:S(2)}, u32[]{:S(2)}) async-start(bf16[32,2,2048]{2,0,1:T(8,128)(2,1)} %copy.94), calls=%async_computation.6 | async-start | bytes 524288 | tf_op jit(solution)/shard_map/all_to_all | solution.py:73
  128.0 330.6 %all-reduce.5.cloned.1.call-start = ((), (), s32[]{:S(2)}) async-start(), calls=%async_computation.9 | async-start | bytes 12582912 | tf_op jit(solution)/shard_map/psum | solution.py:106
  324.5 9.4 %all-to-all-start.3 = ((bf16[32,2,2048]{2,0,1:T(8,128)(2,1)}), bf16[32,2,2048]{2,0,1:T(8,128)(2,1)}, u32[]{:S(2)}, u32[]{:S(2)}) async-start(bf16[32,2,2048]{2,0,1:T(8,128)(2,1)} %copy.86), calls=%async_computation.3 | async-start | bytes 524288 | tf_op jit(solution)/shard_map/all_to_all | solution.py:72
  333.9 9.4 %all-to-all-start.7 = ((bf16[32,2,2048]{2,0,1:T(8,128)(2,1)}), bf16[32,2,2048]{2,0,1:T(8,128)(2,1)}, u32[]{:S(2)}, u32[]{:S(2)}) async-start(bf16[32,2,2048]{2,0,1:T(8,128)(2,1)} %copy.107), calls=%async_computation.7 | async-start | bytes 524288 | tf_op jit(solution)/shard_map/all_to_all | solution.py:72
  (17 other events, 228.1 us)
Sparse Core Ops, SparseCore 0:
  109.1 142.8 all-reduce.2
  319.2 139.3 all-reduce.4
